TPU v7x, 256 devices: a whole 4x4x8 slice. The times are simulated.
256 devices in a mesh: rep: 2 (over z_hi), fsdp: 32 (over y, x, core), tp: 4 (over z_lo).
Axes of the slice: x: 4, y: 4, z: 8 (z_hi: 2, z_lo: 4; z = z_hi * 4 + z_lo), core: 2. Of those that a mesh axis runs over, the one named last changes fastest.
Arguments:
- delta_out: float32 [2, 8, 1792, 1792], P('rep', None, 'tp', 'fsdp'), may hold values from -6 to 6
- delta_down: float32 [2, 8, 4864, 1792], P('rep', None, 'tp', 'fsdp'), may hold values from -6 to 6
- basis: float32 [1792, 64], replicated, may hold values from -0.125 to 0.125
- anchor_out: float32 [8, 4, 448, 1792], P('rep', 'tp', 'fsdp'), may hold values from -6 to 6
- anchor_down: float32 [8, 4, 1216, 1792], P('rep', 'tp', 'fsdp'), may hold values from -6 to 6
- moment_out: float32 [8, 4, 448, 1792], P('rep', 'tp', 'fsdp'), may hold values from -3 to 3
- moment_down: float32 [8, 4, 1216, 1792], P('rep', 'tp', 'fsdp'), may hold values from -3 to 3
Outputs:
- weights_out: bfloat16 [8, 1792, 1792], P(None, 'tp', 'fsdp')
- weights_down: bfloat16 [8, 4864, 1792], P(None, 'tp', 'fsdp')
- anchor_out_new: float32 [8, 4, 448, 1792], P('rep', 'tp', 'fsdp')
- anchor_down_new: float32 [8, 4, 1216, 1792], P('rep', 'tp', 'fsdp')
- moment_out_new: float32 [8, 4, 448, 1792], P('rep', 'tp', 'fsdp')
- moment_down_new: float32 [8, 4, 1216, 1792], P('rep', 'tp', 'fsdp')
All inputs are finite; a program needn't handle non-finite values.
Results may differ from a plain program's by a relative error of at most 0.0055.
Values may be sent and summed in bfloat16 or wider, within the bound.
A program may use at most 64 MiB of HBM per device.

v0:
```python
import jax
import jax.numpy as jnp
from jax import lax
from jax.sharding import PartitionSpec as P

outer_rate = 0.7
nesterov_decay = 0.9


def owner_update(summed, basis, anchor, moment, groups):
    coef = summed / groups
    grad = jnp.einsum("lik,jk->lij", coef, basis, precision=lax.Precision.HIGHEST)
    previous = anchor[:, 0]
    velocity = moment[:, 0]
    moment_new = nesterov_decay * velocity + grad
    anchor_new = previous - outer_rate * (grad + nesterov_decay * moment_new)
    return (anchor_new, moment_new)


def per_device(delta_out, delta_down, basis, anchor_out, anchor_down, moment_out, moment_down):
    groups = lax.axis_size("rep")
    piece_cols = delta_out.shape[3]
    shard_index = lax.axis_index("fsdp")
    basis_rows = lax.dynamic_slice_in_dim(basis, shard_index * piece_cols, piece_cols, 0)
    partial_out = jnp.einsum(
        "lij,jk->lik", delta_out[0], basis_rows, precision=lax.Precision.HIGHEST
    )
    partial_down = jnp.einsum(
        "lij,jk->lik", delta_down[0], basis_rows, precision=lax.Precision.HIGHEST
    )
    layer_sums = (
        lax.psum_scatter(
            partial_out.astype(jnp.bfloat16), "rep", scatter_dimension=0, tiled=True
        ).astype(jnp.float32),
        lax.psum_scatter(
            partial_down.astype(jnp.bfloat16), "rep", scatter_dimension=0, tiled=True
        ).astype(jnp.float32),
    )
    summed_out, summed_down = (
        lax.psum_scatter(
            layer_sums[0].astype(jnp.bfloat16), "fsdp", scatter_dimension=1, tiled=True
        ).astype(jnp.float32),
        lax.psum_scatter(
            layer_sums[1].astype(jnp.bfloat16), "fsdp", scatter_dimension=1, tiled=True
        ).astype(jnp.float32),
    )
    anchor_out_new, moment_out_new = owner_update(summed_out, basis, anchor_out, moment_out, groups)
    anchor_down_new, moment_down_new = owner_update(
        summed_down, basis, anchor_down, moment_down, groups
    )
    rounded_out = anchor_out_new.astype(jnp.bfloat16)
    rounded_down = anchor_down_new.astype(jnp.bfloat16)
    placed_out, placed_down = (
        lax.all_to_all(rounded_out, "fsdp", split_axis=2, concat_axis=1, tiled=True),
        lax.all_to_all(rounded_down, "fsdp", split_axis=2, concat_axis=1, tiled=True),
    )
    weights_out, weights_down = (
        lax.all_gather(placed_out, "rep", axis=0, tiled=True),
        lax.all_gather(placed_down, "rep", axis=0, tiled=True),
    )
    return (
        weights_out,
        weights_down,
        anchor_out_new[:, None],
        anchor_down_new[:, None],
        moment_out_new[:, None],
        moment_down_new[:, None],
    )


def solution(mesh):
    return jax.shard_map(
        per_device,
        mesh=mesh,
        in_specs=(
            P("rep", None, "tp", "fsdp"),
            P("rep", None, "tp", "fsdp"),
            P(),
            P("rep", "tp", "fsdp", None),
            P("rep", "tp", "fsdp", None),
            P("rep", "tp", "fsdp", None),
            P("rep", "tp", "fsdp", None),
        ),
        out_specs=(
            P(None, "tp", "fsdp"),
            P(None, "tp", "fsdp"),
            P("rep", "tp", "fsdp", None),
            P("rep", "tp", "fsdp", None),
            P("rep", "tp", "fsdp", None),
            P("rep", "tp", "fsdp", None),
        ),
        check_vma=False,
    )
```

profile of v0, /device:TPU:32, one launch (start us, length us, event | category | flops | bytes accessed | tf_op | source)
XLA Modules:
  0.0 316.6 jit_solution(11942777162929042482)
XLA Ops:
  7.2 3.2 %fusion.2 = bf16[8,448,64]{1,2,0:T(8,128)(2,1)} fusion(f32[1,8,448,56]{2,3,1,0:T(8,128)} %param.7, f32[1792,64]{0,1:T(8,128)} %param.9, s32[]{:T(128)S(6)} %select_n.3), kind=kOutput, calls=%fused_computation.5 | convolution fusion | flops 154370048 | bytes 1409028 | tf_op jit(solution)/shard_map/lij,jk->lik/dot_general | solution.py:25
  10.5 4.2 %fusion = bf16[8,1216,64]{1,2,0:T(8,128)(2,1)} fusion(f32[1,8,1216,56]{2,3,1,0:T(8,128)S(1)} %copy-done, f32[1792,64]{0,1:T(8,128)} %param.9, s32[]{:T(128)S(6)} %select_n.3), kind=kOutput, calls=%fused_computation.1 | convolution fusion | flops 419004416 | bytes 3457028 | tf_op jit(solution)/shard_map/lij,jk->lik/dot_general | solution.py:28
  14.8 27.6 %reduce-scatter.3.cloned.1.call-done = bf16[4,448,64]{1,2,0:T(8,128)(2,1)} async-done(((bf16[8,448,64]{1,2,0:T(8,128)(2,1)}), bf16[4,448,64]{1,2,0:T(8,128)(2,1)}) %reduce-scatter.3.cloned.1.call-update) | async-done | bytes 229392 | tf_op jit(solution)/shard_map/reduce_scatter | solution.py:32
  42.3 2.0 copy.35
  44.3 43.5 %reduce-scatter.5.cloned.1.call-done = bf16[4,1216,64]{1,2,0:T(8,128)(2,1)} async-done(((bf16[8,1216,64]{1,2,0:T(8,128)(2,1)}), bf16[4,1216,64]{1,2,0:T(8,128)(2,1)}) %reduce-scatter.5.cloned.1.call-update) | async-done | bytes 622608 | tf_op jit(solution)/shard_map/reduce_scatter | solution.py:35
  87.8 3.2 %copy.43 = bf16[4,1216,64]{2,0,1:T(4,128)(2,1)} copy(bf16[4,1216,64]{1,2,0:T(8,128)(2,1)} %reduce-scatter.5.cloned.1.call-done) | data formatting | bytes 1245184 | tf_op jit(solution)/shard_map/reduce_scatter | solution.py:35
  91.1 0.6 copy-done.4
  91.7 0.6 dynamic-slice
  93.0 112.2 %all-reduce.5.cloned.1.call-done = (bf16[4,448,64]{2,0,1:T(4,128)(2,1)}, bf16[4,1216,64]{2,0,1:T(4,128)(2,1)}) async-done(((bf16[4,448,64]{2,0,1:T(4,128)(2,1)}, bf16[4,1216,64]{2,0,1:T(4,128)(2,1)}), (bf16[4,448,64]{2,0,1:T(4,128)(2,1)}, bf16[4,1216,64]{2,0,1:T(4,128)(2,1)})) %all-reduce.5.cloned.1.call-update) | async-done | bytes 851984
  205.2 0.8 convert_multiply_fusion
  205.9 4.2 %fusion.20 = (f32[4,1,38,1792]{3,2,0,1:T(8,128)}, bf16[4,38,1792]{2,1,0:T(8,128)(2,1)}, f32[4,1,38,1792]{3,2,0,1:T(8,128)S(1)}) fusion(f32[4,1,38,1792]{3,1,2,0:T(1,128)} %param.13, f32[4,1,38,1792]{3,1,2,0:T(1,128)} %param.11, f32[1792,64]{0,1:T(8,128)} %param.9, f32[4,38,64]{2,0,1:T(4,128)S(1)} %convert_multiply_fusion), kind=kOutput, calls=%fused_computation.32 | convolution fusion | flops 211097600 | bytes 5400576 | tf_op jit(solution)/shard_map/lik,jk->lij/dot_general | solution.py:12
  210.1 3.6 %copy.46 = bf16[4,38,1792]{1,0,2:T(4,128)(2,1)} copy(bf16[4,38,1792]{2,1,0:T(8,128)(2,1)} %get-tuple-element.27) | data formatting | bytes 1089536 | tf_op jit(solution)/shard_map/convert_element_type | solution.py:52
  213.7 5.8 %reshape.22 = bf16[32,2,4256]{2,1,0:T(2,128)(2,1)} reshape(bf16[1792,4,38]{2,1,0:T(4,128)(2,1)} %bitcast.82) | data formatting | bytes 1089536
  219.4 17.7 %all_to_all.36 = bf16[32,2,4256]{2,1,0:T(2,128)(2,1)} all-to-all(bf16[32,2,4256]{2,1,0:T(2,128)(2,1)} %reshape.22), channel_id=1, replica_groups=mesh['rep'=2,'fsdp'=32,'tp'=4] {'fsdp'}, dimensions={0} | all-to-all | bytes 1089536 | tf_op jit(solution)/shard_map/all_to_all | solution.py:55
  237.2 7.4 %reshape.23 = bf16[1792,4,38]{2,1,0:T(4,128)(2,1)} reshape(bf16[32,2,4256]{2,1,0:T(2,128)(2,1)} %all_to_all.36) | data formatting | bytes 1089536
  244.6 3.5 %copy.100 = bf16[4,38,32,56]{1,2,3,0:T(8,128)(2,1)} copy(bf16[4,38,32,56]{1,0,3,2:T(4,128)(2,1)} %bitcast.80) | data formatting | bytes 1089536 | tf_op jit(solution)/shard_map/all_to_all | solution.py:55
  248.0 4.7 %all_to_all.33 = bf16[4,1216,56]{1,2,0:T(8,128)(2,1)} reshape(bf16[4,32,38,56]{2,1,3,0:T(8,128)(2,1)} %bitcast.81) | data formatting | bytes 1089536 | tf_op jit(solution)/shard_map/all_to_all | solution.py:55
  253.4 1.2 copy.101
  254.5 0.7 convert_multiply_fusion.1
  255.3 2.6 fusion.18
  257.9 3.3 %copy.39 = bf16[4,14,1792]{1,0,2:T(4,128)(2,1)} copy(bf16[4,14,1792]{2,1,0:T(8,128)(2,1)} %get-tuple-element.30) | data formatting | bytes 401408 | tf_op jit(solution)/shard_map/convert_element_type | solution.py:51
  261.2 4.8 %reshape.20 = bf16[32,2,1568]{2,1,0:T(2,128)(2,1)} reshape(bf16[1792,4,14]{2,1,0:T(4,128)(2,1)} %bitcast.83) | data formatting | bytes 401408
  266.1 4.8 %all-to-all-start = ((bf16[32,2,1568]{2,1,0:T(2,128)(2,1)}), bf16[32,2,1568]{2,1,0:T(2,128)(2,1)}, u32[]{:S(2)}, u32[]{:S(2)}) async-start(bf16[32,2,1568]{2,1,0:T(2,128)(2,1)} %reshape.20), calls=%async_computation.1 | async-start | bytes 425984 | tf_op jit(solution)/shard_map/all_to_all | solution.py:54
  270.8 3.4 %copy.50 = f32[4,1,38,1792]{3,1,2,0:T(1,128)} copy(f32[4,1,38,1792]{3,2,0,1:T(8,128)} %get-tuple-element.26) | data formatting | bytes 2179072
  274.2 2.1 copy.52
  276.3 1.2 copy.49
  277.5 1.2 copy.51
  279.0 6.8 %reshape.21 = bf16[1792,4,14]{2,1,0:T(4,128)(2,1)} reshape(bf16[32,2,1568]{2,1,0:T(2,128)(2,1)} %all-to-all-done) | data formatting | bytes 401408
  285.8 3.4 %copy.53 = bf16[4,14,32,56]{3,2,0,1:T(8,128)(2,1)S(1)} copy(bf16[4,14,32,56]{1,0,3,2:T(4,128)(2,1)} %bitcast.84) | data formatting | bytes 401408 | tf_op jit(solution)/shard_map/all_to_all | solution.py:54
  289.7 17.3 %all_gather.6 = bf16[8,448,56]{1,2,0:T(8,128)(2,1)S(1)} all-gather(bf16[4,448,56]{1,2,0:T(8,128)(2,1)S(1)} %copy.42), channel_id=1, replica_groups=mesh['rep'=2,'fsdp'=32,'tp'=4] {'rep'}, dimensions={0}, use_global_device_ids=true | all-gather | bytes 602112 | tf_op jit(solution)/shard_map/all_gather | solution.py:58
  307.0 0.8 copy.106
  307.8 2.3 copy.107
  (21 shorter events, 1.1 us)
Async XLA Ops:
  7.2 3.3 %copy-start = (f32[1,8,1216,56]{2,3,1,0:T(8,128)S(1)}, f32[1,8,1216,56]{2,3,1,0:T(8,128)}, u32[]{:S(2)}) copy-start(f32[1,8,1216,56]{2,3,1,0:T(8,128)} %param.8) | copy-start | bytes 6537220
  7.2 35.2 %reduce-scatter.3.cloned.1.call-start = ((), (), s32[]{:S(2)}) async-start(), calls=%async_computation.4 | async-start | bytes 786432 | tf_op jit(solution)/shard_map/reduce_scatter | solution.py:32
  10.4 77.4 %reduce-scatter.5.cloned.1.call-start = ((), (), s32[]{:S(2)}) async-start(), calls=%async_computation.5 | async-start | bytes 1966080 | tf_op jit(solution)/shard_map/reduce_scatter | solution.py:35
  14.7 190.4 %all-reduce.5.cloned.1.call-start = ((), (), s32[]{:S(2)}) async-start(), calls=%async_computation.7 | async-start | bytes 3407872
  91.0 0.7 copy-start.4
  91.1 215.9 %all-gather.2.cloned.1.call-start = ((), (), s32[]{:S(2)}) async-start(), calls=%async_computation.6 | async-start | bytes 1720320 | tf_op jit(solution)/shard_map/all_gather | solution.py:59
  253.4 1.9 copy-start.1
  266.1 12.9 %all-to-all-start = ((bf16[32,2,1568]{2,1,0:T(2,128)(2,1)}), bf16[32,2,1568]{2,1,0:T(2,128)(2,1)}, u32[]{:S(2)}, u32[]{:S(2)}) async-start(bf16[32,2,1568]{2,1,0:T(2,128)(2,1)} %reshape.20), calls=%async_computation.1 | async-start | bytes 425984 | tf_op jit(solution)/shard_map/all_to_all | solution.py:54
  274.2 2.1 copy-start.3
  274.2 3.3 %copy-start.2 = (f32[4,1,14,1792]{3,2,0,1:T(8,128)S(1)}, f32[4,1,14,1792]{3,2,0,1:T(8,128)}, u32[]{:S(2)}) copy-start(f32[4,1,14,1792]{3,2,0,1:T(8,128)} %get-tuple-element.31) | copy-start | bytes 1204228
Sparse Core Ops, SparseCore 0:
  11.1 31.2 reduce-scatter.2
  45.0 42.7 reduce-scatter.4
  91.8 113.3 all-reduce.4
  252.8 40.9 all-gather.1
where the time goes:
time: 318 us; the launch traced here: 317 us
  waiting for transfers between devices  184 us (58%)
  local copies, waits for them, and re-layouts  62.2 us (20%)
  blocking collectives  35 us (11%)
  between operations  15.2 us (5%)
  matrix products  14.1 us (4%)
  starting transfers between devices  4.95 us (2%)
    unnamed x5, waiting for transfers between devices  112 us
    reduce_scatter x1, waiting for transfers between devices, per_device(): lax.psum_scatter(partial_down.astype(jnp.bfloat16), 'rep', scatter_dimens...  43.5 us
    unnamed x22, local copies, waits for them, and re-layouts  38 us
    reduce_scatter x1, waiting for transfers between devices, per_device(): lax.psum_scatter(partial_out.astype(jnp.bfloat16), 'rep', scatter_dimensi...  27.6 us
    all_to_all x1, blocking collectives, per_device(): lax.all_to_all(rounded_down, 'fsdp', split_axis=2, concat_axis=1, tiled=T...  17.7 us
    all_gather x1, blocking collectives, per_device(): lax.all_gather(placed_out, 'rep', axis=0, tiled=True)  17.3 us
    all_to_all x2, local copies, waits for them, and re-layouts, per_device(): lax.all_to_all(rounded_down, 'fsdp', split_axis=2, concat_axis=1, tiled=T...  8.1 us
    dot_general x2, matrix products, owner_update(): jnp.einsum('lik,jk->lij', coef, basis, precision=lax.Precision.HIGHEST)  6.77 us
  transfers between devices with their start and end apart: 5, of which 4 were waited for; matrix products, arithmetic and copies ran while one was open for 12% of the time, Pallas kernels for 0%

commit v1 on v0

--- a/solution.py
+++ b/solution.py
@@ -5,6 +5,12 @@
 
 outer_rate = 0.7
 nesterov_decay = 0.9
+
+
+def stacked_exchange(block, axis, split, join):
+    shards = jnp.split(block, lax.axis_size(axis), axis=split)
+    received = lax.all_to_all(jnp.stack(shards), axis, 0, 0)
+    return jnp.concatenate(received, axis=join)
 
 
 def owner_update(summed, basis, anchor, moment, groups):
@@ -52,7 +58,7 @@
     rounded_down = anchor_down_new.astype(jnp.bfloat16)
     placed_out, placed_down = (
         lax.all_to_all(rounded_out, "fsdp", split_axis=2, concat_axis=1, tiled=True),
-        lax.all_to_all(rounded_down, "fsdp", split_axis=2, concat_axis=1, tiled=True),
+        stacked_exchange(rounded_down, "fsdp", 2, 1),
     )
     weights_out, weights_down = (
         lax.all_gather(placed_out, "rep", axis=0, tiled=True),

time: 318 us -> 303 us (0.953)
  local copies, waits for them, and re-layouts: 62.2 us -> 48.9 us
    all_to_all x2 -> x0, local copies, waits for them, and re-layouts: 8.1 us -> none  [per_device(): lax.all_to_all(rounded_down, 'fsdp', split_axis=2, concat_axis=1, tiled=T...]
    unnamed x22 -> x57, local copies, waits for them, and re-layouts: 38 us -> 34.5 us
    convert_element_type x1 -> x0, local copies, waits for them, and re-layouts: 3.56 us -> none  [per_device(): rounded_down = anchor_down_new.astype(jnp.bfloat16)]
  transfers between devices with their start and end apart: 5 -> 5, of which waited for: 4 -> 3; matrix products, arithmetic and copies ran while one was open for 12% -> 12% of each run, Pallas kernels for 0% -> 0%
where the time goes in v1:
time: 303 us; the launch traced here: 302 us
  waiting for transfers between devices  184 us (61%)
  local copies, waits for them, and re-layouts  48.9 us (16%)
  blocking collectives  34.6 us (11%)
  between operations  15.4 us (5%)
  matrix products  12.3 us (4%)
  starting transfers between devices  5.09 us (2%)
    unnamed x5, waiting for transfers between devices  112 us
    reduce_scatter x1, waiting for transfers between devices, per_device(): lax.psum_scatter(partial_down.astype(jnp.bfloat16), 'rep', scatter_dimens...  43.5 us
    unnamed x57, local copies, waits for them, and re-layouts  34.5 us
    reduce_scatter x1, waiting for transfers between devices, per_device(): lax.psum_scatter(partial_out.astype(jnp.bfloat16), 'rep', scatter_dimensi...  28.4 us
    all_to_all x1, blocking collectives, stacked_exchange(): received = lax.all_to_all(jnp.stack(shards), axis, 0, 0)  17.7 us
    all_gather x1, blocking collectives, per_device(): lax.all_gather(placed_out, 'rep', axis=0, tiled=True)  16.9 us
  transfers between devices with their start and end apart: 5, of which 3 were waited for; matrix products, arithmetic and copies ran while one was open for 12% of the time, Pallas kernels for 0%

profile of v1, /device:TPU:32, one launch (start us, length us, event | category | flops | bytes accessed | tf_op | source)
XLA Modules:
  0.0 302.0 jit_solution(9035037345845403970)
XLA Ops:
  7.2 3.2 %fusion.2 = bf16[8,448,64]{1,2,0:T(8,128)(2,1)} fusion(f32[1,8,448,56]{2,3,1,0:T(8,128)} %param.7, f32[1792,64]{0,1:T(8,128)} %param.9, s32[]{:T(128)S(6)} %select_n.3), kind=kOutput, calls=%fused_computation.4 | convolution fusion | flops 154370048 | bytes 1409028 | tf_op jit(solution)/shard_map/lij,jk->lik/dot_general | solution.py:31
  10.5 3.3 %fusion = bf16[8,1216,64]{1,2,0:T(8,128)(2,1)} fusion(f32[1,8,1216,56]{2,3,1,0:T(8,128)S(1)} %copy-done, f32[1792,64]{0,1:T(8,128)S(1)} %copy-done.3, s32[]{:T(128)S(6)} %select_n.3), kind=kOutput, calls=%fused_computation.1 | convolution fusion | flops 419004416 | bytes 3571716 | tf_op jit(solution)/shard_map/lij,jk->lik/dot_general | solution.py:34
  13.9 28.4 %reduce-scatter.3.cloned.1.call-done = bf16[4,448,64]{1,2,0:T(8,128)(2,1)} async-done(((bf16[8,448,64]{1,2,0:T(8,128)(2,1)}), bf16[4,448,64]{1,2,0:T(8,128)(2,1)}) %reduce-scatter.3.cloned.1.call-update) | async-done | bytes 229392 | tf_op jit(solution)/shard_map/reduce_scatter | solution.py:38
  42.3 2.0 copy.34
  44.3 43.5 %reduce-scatter.5.cloned.1.call-done = bf16[4,1216,64]{1,2,0:T(8,128)(2,1)} async-done(((bf16[8,1216,64]{1,2,0:T(8,128)(2,1)}), bf16[4,1216,64]{1,2,0:T(8,128)(2,1)}) %reduce-scatter.5.cloned.1.call-update) | async-done | bytes 622608 | tf_op jit(solution)/shard_map/reduce_scatter | solution.py:41
  87.8 3.2 %copy.42 = bf16[4,1216,64]{2,0,1:T(4,128)(2,1)} copy(bf16[4,1216,64]{1,2,0:T(8,128)(2,1)} %reduce-scatter.5.cloned.1.call-done) | data formatting | bytes 1245184 | tf_op jit(solution)/shard_map/reduce_scatter | solution.py:41
  91.1 0.6 copy-done.6
  91.7 0.6 dynamic-slice
  93.0 112.2 %all-reduce.5.cloned.1.call-done = (bf16[4,448,64]{2,0,1:T(4,128)(2,1)}, bf16[4,1216,64]{2,0,1:T(4,128)(2,1)}) async-done(((bf16[4,448,64]{2,0,1:T(4,128)(2,1)}, bf16[4,1216,64]{2,0,1:T(4,128)(2,1)}), (bf16[4,448,64]{2,0,1:T(4,128)(2,1)}, bf16[4,1216,64]{2,0,1:T(4,128)(2,1)})) %all-reduce.5.cloned.1.call-update) | async-done | bytes 851984
  205.2 0.8 convert_multiply_fusion
  206.0 4.2 %fusion.20 = (f32[4,1,38,1792]{3,2,0,1:T(8,128)}, bf16[4,38,1792]{2,1,0:T(8,128)(2,1)S(1)}, f32[4,1,38,1792]{3,2,0,1:T(8,128)}) fusion(f32[4,1,38,1792]{3,1,2,0:T(1,128)} %param.13, f32[4,1,38,1792]{3,1,2,0:T(1,128)} %param.11, f32[1792,64]{0,1:T(8,128)S(1)} %copy-done.3, f32[4,38,64]{2,0,1:T(4,128)S(1)} %convert_multiply_fusion), kind=kOutput, calls=%fused_computation.95 | convolution fusion | flops 211097600 | bytes 5400576 | tf_op jit(solution)/shard_map/lik,jk->lij/dot_general | solution.py:18
  213.1 0.5 copy.98
  213.5 2.8 reshape.30
  216.4 17.7 %all_to_all.23 = bf16[32,2,4256]{2,1,0:T(2,128)(2,1)} all-to-all(bf16[32,2,4256]{2,1,0:T(2,128)(2,1)} %reshape.30), channel_id=1, replica_groups=mesh['rep'=2,'fsdp'=32,'tp'=4] {'fsdp'}, dimensions={0} | all-to-all | bytes 1089536 | tf_op jit(solution)/shard_map/all_to_all | solution.py:12
  234.1 3.5 %reshape.31 = bf16[32,38,4,56]{3,2,1,0:T(4,128)(2,1)S(1)} reshape(bf16[32,2,4256]{2,1,0:T(2,128)(2,1)} %all_to_all.23) | data formatting | bytes 1089536
  237.6 2.4 copy.52
  240.7 1.1 copy.97
  241.8 0.7 convert_multiply_fusion.1
  242.6 1.6 fusion.18
  244.1 2.4 copy.38
  246.5 4.8 %reshape.28 = bf16[32,2,1568]{2,1,0:T(2,128)(2,1)} reshape(bf16[1792,4,14]{2,1,0:T(4,128)(2,1)} %bitcast.204) | data formatting | bytes 401408
  251.3 4.9 %all-to-all-start = ((bf16[32,2,1568]{2,1,0:T(2,128)(2,1)}), bf16[32,2,1568]{2,1,0:T(2,128)(2,1)}, u32[]{:S(2)}, u32[]{:S(2)}) async-start(bf16[32,2,1568]{2,1,0:T(2,128)(2,1)} %reshape.28), calls=%async_computation.1 | async-start | bytes 425984 | tf_op jit(solution)/shard_map/all_to_all | solution.py:60
  256.2 2.2 copy.47
  258.4 2.2 copy.49
  260.6 2.1 copy.48
  262.7 2.1 copy.50
  264.8 6.7 %reshape.29 = bf16[1792,4,14]{2,1,0:T(4,128)(2,1)} reshape(bf16[32,2,1568]{2,1,0:T(2,128)(2,1)} %all-to-all-done) | data formatting | bytes 401408
  271.5 3.4 %copy.51 = bf16[4,14,32,56]{3,2,0,1:T(8,128)(2,1)S(1)} copy(bf16[4,14,32,56]{1,0,3,2:T(4,128)(2,1)} %bitcast.205) | data formatting | bytes 401408 | tf_op jit(solution)/shard_map/all_to_all | solution.py:60
  275.1 0.3 copy.41
  275.4 16.9 %all_gather.6 = bf16[8,448,56]{1,2,0:T(8,128)(2,1)S(1)} all-gather(bf16[4,448,56]{1,2,0:T(8,128)(2,1)S(1)} %copy.41), channel_id=1, replica_groups=mesh['rep'=2,'fsdp'=32,'tp'=4] {'rep'}, dimensions={0}, use_global_device_ids=true | all-gather | bytes 602112 | tf_op jit(solution)/shard_map/all_gather | solution.py:64
  292.3 0.8 copy.134
  293.1 2.3 copy.135
  (56 shorter events, 3.3 us)
Async XLA Ops:
  7.2 3.3 %copy-start = (f32[1,8,1216,56]{2,3,1,0:T(8,128)S(1)}, f32[1,8,1216,56]{2,3,1,0:T(8,128)}, u32[]{:S(2)}) copy-start(f32[1,8,1216,56]{2,3,1,0:T(8,128)} %param.8) | copy-start | bytes 6537220
  7.2 3.3 %copy-start.3 = (f32[1792,64]{0,1:T(8,128)S(1)}, f32[1792,64]{0,1:T(8,128)}, u32[]{:S(2)}) copy-start(f32[1792,64]{0,1:T(8,128)} %param.9) | copy-start | bytes 1376260
  7.2 35.2 %reduce-scatter.3.cloned.1.call-start = ((), (), s32[]{:S(2)}) async-start(), calls=%async_computation.4 | async-start | bytes 786432 | tf_op jit(solution)/shard_map/reduce_scatter | solution.py:38
  10.5 77.4 %reduce-scatter.5.cloned.1.call-start = ((), (), s32[]{:S(2)}) async-start(), calls=%async_computation.5 | async-start | bytes 1966080 | tf_op jit(solution)/shard_map/reduce_scatter | solution.py:41
  13.9 191.3 %all-reduce.5.cloned.1.call-start = ((), (), s32[]{:S(2)}) async-start(), calls=%async_computation.7 | async-start | bytes 3407872
  91.1 0.7 copy-start.6
  91.1 201.2 %all-gather.2.cloned.1.call-start = ((), (), s32[]{:S(2)}) async-start(), calls=%async_computation.6 | async-start | bytes 1720320 | tf_op jit(solution)/shard_map/all_gather | solution.py:65
  240.0 2.6 copy-start.4
  240.0 2.6 copy-start.5
  251.3 9.3 %copy-start.2 = (f32[4,1,38,1792]{3,2,0,1:T(8,128)S(1)}, f32[4,1,38,1792]{3,2,0,1:T(8,128)}, u32[]{:S(2)}) copy-start(f32[4,1,38,1792]{3,2,0,1:T(8,128)} %get-tuple-element.26) | copy-start | bytes 3268612
  251.3 13.5 %all-to-all-start = ((bf16[32,2,1568]{2,1,0:T(2,128)(2,1)}), bf16[32,2,1568]{2,1,0:T(2,128)(2,1)}, u32[]{:S(2)}, u32[]{:S(2)}) async-start(bf16[32,2,1568]{2,1,0:T(2,128)(2,1)} %reshape.28), calls=%async_computation.1 | async-start | bytes 425984 | tf_op jit(solution)/shard_map/all_to_all | solution.py:60
  260.6 2.1 copy-start.1
Sparse Core Ops, SparseCore 0:
  11.1 31.2 reduce-scatter.2
  45.0 42.7 reduce-scatter.4
  91.8 113.3 all-reduce.4
  240.1 40.9 all-gather.1
